TPU v7x, 128 devices: a whole 4x4x4 slice. The times are simulated.
128 devices in a mesh: slab: 32 (over y, z, core), col: 4 (over x).
Axes of the slice: x: 4, y: 4, z: 4, core: 2. Of those that a mesh axis runs over, the one named last changes fastest.
Arguments:
- input_map: float32 [64, 64, 192, 128], P('col', 'slab'), may hold values from -24 to 24
- output_map: float32 [64, 64, 192, 128], P('col', 'slab'), may hold values from -24 to 24
- region_ids: int32 [64, 192, 128], P('slab'), may hold values from 0 to 7
- region_cond: float32 [8], replicated, may hold values from 0.3 to 3
- shift_ids: int32 [2], replicated, may hold values from 0 to 7
Outputs:
- ctrl_factor: float32 [2, 64, 64, 192, 128], P(None, None, 'slab', 'col')
- obsv_factor: float32 [2, 64, 64, 192, 128], P(None, None, 'slab', 'col')
- cross_gram: float32 [128, 128], P('slab', 'col')
All inputs are finite; a program needn't handle non-finite values.
Results may differ from a plain program's by a relative error of at most 0.000098.
Values sent between devices are 32-bit elements; how exact they have to be, the bound alone decides.
A program may use at most 192 MiB of HBM per device.

v0:
```python
import math
import jax
import jax.numpy as jnp
from jax import lax
from jax.sharding import PartitionSpec as P

ADI = 2
STEPS = 3


def extended(block, sides, width):
    for axis, dim in sides:
        count = lax.axis_size(axis)
        forward = [(i, i + 1) for i in range(count - 1)]
        backward = [(target, source) for source, target in forward]
        low = lax.ppermute(
            lax.slice_in_dim(block, block.shape[dim] - width, None, axis=dim), axis, forward
        )
        high = lax.ppermute(lax.slice_in_dim(block, 0, width, axis=dim), axis, backward)
        block = jnp.concatenate([low, block, high], axis=dim)
    return block


def lookup(region_ids, region_cond):
    summed = jnp.zeros(region_ids.shape, jnp.float32)
    for region in range(region_cond.shape[0]):
        summed = summed + jnp.where(region_ids == region, region_cond[region], jnp.float32(0.0))
    return summed


def conduction(field_in, cond_ext):
    centre = field_in[:, 1:-1]
    cond_mid = cond_ext[1:-1]
    summed = 0.5 * (cond_mid + cond_ext[2:]) * (centre - field_in[:, 2:])
    summed = summed + 0.5 * (cond_mid + cond_ext[:-2]) * (centre - field_in[:, :-2])
    cond_y = jnp.pad(cond_mid, ((0, 0), (1, 1), (0, 0)))
    field_y = jnp.pad(centre, ((0, 0), (0, 0), (1, 1), (0, 0)))
    summed = summed + 0.5 * (cond_mid + cond_y[:, 2:]) * (centre - field_y[:, :, 2:])
    summed = summed + 0.5 * (cond_mid + cond_y[:, :-2]) * (centre - field_y[:, :, :-2])
    cond_z = jnp.pad(cond_mid, ((0, 0), (0, 0), (1, 1)))
    field_z = jnp.pad(centre, ((0, 0), (0, 0), (0, 0), (1, 1)))
    summed = summed + 0.5 * (cond_mid + cond_z[:, :, 2:]) * (centre - field_z[:, :, :, 2:])
    summed = summed + 0.5 * (cond_mid + cond_z[:, :, :-2]) * (centre - field_z[:, :, :, :-2])
    return summed


def bounds(shift_val, cond_max):
    high_eig = shift_val + 12.0 * cond_max
    mid_eig = 0.5 * (high_eig + shift_val)
    half_span = 0.5 * (high_eig - shift_val)
    return (mid_eig, half_span, mid_eig / half_span)


def solve_slabs(right_side, shift_val, cond_max, cond_ext):
    mid_eig, half_span, ratio_eig = bounds(shift_val, cond_max)
    rho_now = 1.0 / ratio_eig
    solution = jnp.zeros_like(right_side)
    residual = right_side
    direction = right_side / mid_eig
    for sweep_idx in range(STEPS - 1):
        solution = solution + direction
        padded = extended(direction, (("slab", 1),), 1)
        applied = conduction(padded, cond_ext) + shift_val * direction
        residual = residual - applied
        rho_next = 1.0 / (2.0 * ratio_eig - rho_now)
        direction = rho_next * rho_now * direction + 2.0 * rho_next / half_span * residual
        rho_now = rho_next
    return solution + direction


def run_segments(stacked, shifts, solver):
    factors = []
    current = stacked
    for segment_idx in range(ADI):
        shift_val = shifts[segment_idx]
        if segment_idx == 0:
            current = solver(stacked, shift_val)
        else:
            current = current - (shifts[segment_idx - 1] + shift_val) * solver(current, shift_val)
        factors.append(jnp.sqrt(2.0 * shift_val) * current)
    return jnp.stack(factors)


def body(input_map, output_map, region_ids, region_cond, shift_ids):
    col_local = input_map.shape[0]
    local_x = input_map.shape[1]
    cond_cells = lookup(region_ids, region_cond)
    cond_max = jnp.max(region_cond)
    shifts = 0.25 * jnp.exp2(shift_ids.astype(jnp.float32))
    total_x = local_x * lax.axis_size("slab")
    stacked = jnp.concatenate([input_map, output_map], 0)
    cond_ext = extended(cond_cells, (("slab", 0),), 1)
    factor_stack = run_segments(
        stacked, shifts, lambda rhs, shift_val: solve_slabs(rhs, shift_val, cond_max, cond_ext)
    )
    ctrl_local = factor_stack[:, :col_local]
    obsv_local = factor_stack[:, col_local:]
    ctrl_cols, obsv_cols = (
        lax.all_to_all(ctrl_local, "col", split_axis=3, concat_axis=1, tiled=True),
        lax.all_to_all(obsv_local, "col", split_axis=3, concat_axis=1, tiled=True),
    )
    row_count = ctrl_cols.shape[0] * ctrl_cols.shape[1]
    ctrl_flat = ctrl_cols.reshape(row_count, -1)
    obsv_flat = obsv_cols.reshape(row_count, -1)
    partial_value = lax.dot_general(
        ctrl_flat,
        obsv_flat,
        (((1,), (1,)), ((), ())),
        precision=lax.Precision.HIGHEST,
        preferred_element_type=jnp.float32,
    )
    cells_total = total_x * region_ids.shape[1] * region_ids.shape[2]
    norm_scale = 1.0 / math.sqrt(cells_total)
    slab_count = lax.axis_size("slab")
    col_count = lax.axis_size("col")
    tile_rows = row_count // slab_count
    tile_cols = row_count // col_count
    col_parts = partial_value.reshape(row_count, col_count, tile_cols).transpose(1, 0, 2)
    col_sum = jnp.sum(lax.all_to_all(col_parts, "col", 0, 0, tiled=True), axis=0)
    row_parts = col_sum.reshape(slab_count, tile_rows, tile_cols)
    own_tile = jnp.sum(lax.all_to_all(row_parts, "slab", 0, 0, tiled=True), axis=0)
    return (ctrl_cols, obsv_cols, own_tile * norm_scale)


def solution(mesh):
    placed = (
        P("col", "slab", None, None),
        P("col", "slab", None, None),
        P("slab", None, None),
        P(),
        P(),
    )
    return jax.shard_map(
        body,
        mesh=mesh,
        in_specs=placed,
        out_specs=(
            P(None, None, "slab", "col", None),
            P(None, None, "slab", "col", None),
            P("slab", "col"),
        ),
        check_vma=False,
    )
```

profile of v0, /device:TPU:1, one launch (start us, length us, event | category | flops | bytes accessed | tf_op | source)
XLA Modules:
  0.0 515.3 jit_solution(2384388008624997984)
XLA Ops:
  5.3 3.9 constant_dynamic-update-slice_fusion.1
  14.4 3.3 fusion.105
  18.9 3.3 collective-permute-start.1
  22.3 3.5 collective-permute-start.3
  26.5 5.0 select_add_fusion
  37.9 22.1 %collective-permute-done = f32[1,192,128]{2,1,0:T(8,128)S(1)} collective-permute-done((f32[1,192,128]{2,1,0:T(8,128)S(1)}, f32[1,192,128]{2,1,0:T(8,128)S(1)}, u32[]{:S(2)}, u32[]{:S(2)}) %collective-permute-start) | collective-permute-done | bytes 98336 | tf_op jit(solution)/shard_map/ppermute | solution.py:19
  61.4 23.3 %multiply_add_fusion.1 = (f32[32,2,192,128]{3,2,1,0:T(8,128)S(1)}, f32[32,2,192,128]{3,2,1,0:T(8,128)}) fusion(f32[32,2,192,128]{3,2,1,0:T(8,128)} %copy-done.1, f32[]{:T(128)S(6)} %div.53, f32[]{:T(128)S(6)} %mul.348, f32[32,2,192,128]{3,2,1,0:T(8,128)} %constant_dynamic-update-slice_fusion, f32[]{:T(128)} %bitcast, ...), kind=kLoop, calls=%fused_computation.116 | loop fusion | flops 39321600 | bytes 32636940 | tf_op jit(solution)/shard_map/add | solution.py:66
  84.8 3.3 fusion.104
  91.3 4.4 collective-permute-start.5
  97.1 31.9 %collective-permute-done.4 = f32[32,1,192,128]{3,2,1,0:T(8,128)} collective-permute-done((f32[32,1,192,128]{3,2,1,0:T(8,128)}, f32[32,1,192,128]{3,2,1,0:T(8,128)}, u32[]{:S(2)}, u32[]{:S(2)}) %collective-permute-start.4) | collective-permute-done | bytes 3145760 | tf_op jit(solution)/shard_map/ppermute | solution.py:19
  130.2 25.9 %broadcast_divide_fusion = (f32[32,2,192,128]{3,2,1,0:T(8,128)S(1)}, f32[32,2,192,128]{3,2,1,0:T(8,128)}) fusion(f32[]{:T(128)S(6)} %mul.391, f32[32,2,192,128]{3,2,1,0:T(8,128)} %get-tuple-element.8, f32[32,2,192,128]{3,2,1,0:T(8,128)} %copy-done.3, f32[]{:T(128)} %bitcast, f32[2,192,128]{2,1,0:T(8,128)S(1)} %get-tuple-element.29, ...), kind=kLoop, calls=%fused_computation.117 | loop fusion | flops 45613056 | bytes 38928404 | tf_op jit(solution)/shard_map/div | solution.py:59
  156.1 3.8 fusion.103
  162.6 4.4 collective-permute-start.7
  168.5 31.8 %collective-permute-done.6 = f32[32,1,192,128]{3,2,1,0:T(8,128)} collective-permute-done((f32[32,1,192,128]{3,2,1,0:T(8,128)}, f32[32,1,192,128]{3,2,1,0:T(8,128)}, u32[]{:S(2)}, u32[]{:S(2)}) %collective-permute-start.6) | collective-permute-done | bytes 3145760 | tf_op jit(solution)/shard_map/ppermute | solution.py:19
  201.5 26.6 %multiply_add_fusion = (f32[32,2,192,128]{3,2,1,0:T(8,128)S(1)}, f32[32,2,192,128]{3,2,1,0:T(8,128)}, f32[1,32,2,192,128]{4,3,2,1,0:T(8,128)}) fusion(f32[]{:T(128)S(6)} %div.61, f32[]{:T(128)S(6)} %mul.394, f32[32,2,192,128]{3,2,1,0:T(8,128)} %get-tuple-element.6, f32[]{:T(128)S(6)} %mul.391, f32[32,2,192,128]{3,2,1,0:T(8,128)} %copy-done.2, f32[]{:T(128)} %bitcast.10, ...), kind=kLoop, calls=%fused_computation.114 | loop fusion | flops 42467328 | bytes 38928404 | tf_op jit(solution)/shard_map/add | solution.py:66
  228.1 3.8 fusion.102
  234.6 4.6 collective-permute-start.9
  241.3 31.0 %collective-permute-done.8 = f32[32,1,192,128]{3,2,1,0:T(8,128)} collective-permute-done((f32[32,1,192,128]{3,2,1,0:T(8,128)}, f32[32,1,192,128]{3,2,1,0:T(8,128)}, u32[]{:S(2)}, u32[]{:S(2)}) %collective-permute-start.8) | collective-permute-done | bytes 3145760 | tf_op jit(solution)/shard_map/ppermute | solution.py:19
  273.5 27.1 %fusion.47 = f32[1,32,2,192,128]{4,3,2,1,0:T(8,128)S(1)} fusion(f32[32,2,192,128]{3,2,1,0:T(8,128)} %get-tuple-element.6, f32[32,2,192,128]{3,2,1,0:T(8,128)} %get-tuple-element.4, f32[32,2,192,128]{3,2,1,0:T(8,128)} %copy-done, f32[32,1,192,128]{3,2,1,0:T(8,128)} %collective-permute-done.9, f32[32,1,192,128]{3,2,1,0:T(8,128)} %collective-permute-done.8, ...), kind=kLoop, calls=%fused_computation.65 | loop fusion | flops 48758784 | bytes 32636952 | tf_op jit(solution)/shard_map/stack | solution.py:81
  303.7 7.5 %copy.35 = f32[2,16,2,192,128]{4,2,1,0,3:T(2,128)} copy(f32[2,16,2,192,128]{4,3,2,1,0:T(8,128)S(1)} %get-tuple-element.9) | data formatting | bytes 12582912 | tf_op jit(solution)/shard_map/slice | solution.py:97
  311.2 5.2 %all-to-all-start.1 = ((f32[2,16,2,192,128]{4,2,1,0,3:T(2,128)}), f32[2,16,2,192,128]{4,2,1,0,3:T(2,128)}, u32[]{:S(2)}, u32[]{:S(2)}) async-start(f32[2,16,2,192,128]{4,2,1,0,3:T(2,128)} %copy.35), calls=%async_computation.1 | async-start | bytes 12582912 | tf_op jit(solution)/shard_map/all_to_all | solution.py:100
  316.5 10.3 %copy.33 = f32[2,16,2,192,128]{4,2,1,0,3:T(2,128)} copy(f32[2,16,2,192,128]{4,3,2,1,0:T(8,128)} %get-tuple-element.10) | data formatting | bytes 12582912 | tf_op jit(solution)/shard_map/slice | solution.py:96
  326.8 51.0 %all-to-all-done.1 = f32[2,16,2,192,128]{4,2,1,0,3:T(2,128)} async-done(((f32[2,16,2,192,128]{4,2,1,0,3:T(2,128)}), f32[2,16,2,192,128]{4,2,1,0,3:T(2,128)}, u32[]{:S(2)}, u32[]{:S(2)}) %all-to-all-start.1) | async-done | bytes 6291488 | tf_op jit(solution)/shard_map/all_to_all | solution.py:100
  377.8 5.5 %all-to-all-start = ((f32[2,16,2,192,128]{4,2,1,0,3:T(2,128)}), f32[2,16,2,192,128]{4,2,1,0,3:T(2,128)}, u32[]{:S(2)}, u32[]{:S(2)}) async-start(f32[2,16,2,192,128]{4,2,1,0,3:T(2,128)} %copy.33), calls=%async_computation | async-start | bytes 12582912 | tf_op jit(solution)/shard_map/all_to_all | solution.py:99
  383.2 9.0 %copy.42 = f32[2,16,2,4,48,128]{5,4,2,1,3,0:T(8,128)} copy(f32[2,16,2,4,48,128]{5,2,1,0,4,3:T(2,128)} %bitcast.15) | data formatting | bytes 12582912 | tf_op jit(solution)/shard_map/all_to_all | solution.py:100
  392.3 7.4 %dot_general.5 = f32[4,32,12288]{2,1,0:T(8,128)} reshape(f32[2,4,16,2,48,128]{5,4,3,2,1,0:T(8,128)} %bitcast.35) | data formatting | bytes 12582912 | tf_op jit(solution)/shard_map/dot_general | solution.py:105
  399.7 25.4 %all-to-all-done = f32[2,16,2,192,128]{4,2,1,0,3:T(2,128)} async-done(((f32[2,16,2,192,128]{4,2,1,0,3:T(2,128)}), f32[2,16,2,192,128]{4,2,1,0,3:T(2,128)}, u32[]{:S(2)}, u32[]{:S(2)}) %all-to-all-start) | async-done | bytes 6291488 | tf_op jit(solution)/shard_map/all_to_all | solution.py:99
  425.1 9.0 %copy.43 = f32[2,16,2,4,48,128]{5,4,2,1,3,0:T(8,128)} copy(f32[2,16,2,4,48,128]{5,2,1,0,4,3:T(2,128)} %bitcast.12) | data formatting | bytes 12582912 | tf_op jit(solution)/shard_map/all_to_all | solution.py:99
  434.1 7.5 %reshape.26 = f32[128,12288,1]{1,0,2:T(8,128)} reshape(f32[2,4,16,2,48,128]{5,4,3,2,1,0:T(8,128)} %bitcast.37) | data formatting | bytes 12582912 | tf_op jit(solution)/shard_map/reshape | solution.py:103
  441.6 8.2 %convolution_bitcast_fusion = f32[4,128,32]{1,2,0:T(8,128)S(1)} fusion(f32[128,12288,1]{1,0,2:T(8,128)} %reshape.26, f32[4,32,12288]{2,1,0:T(8,128)} %dot_general.5), kind=kOutput, calls=%fused_computation.119 | convolution fusion | flops 2415919104 | bytes 12648448 | tf_op jit(solution)/shard_map/dot_general | solution.py:105
  449.8 6.8 %all_to_all.46 = f32[4,128,32]{1,2,0:T(8,128)S(1)} all-to-all(f32[4,128,32]{1,2,0:T(8,128)S(1)} %convolution_bitcast_fusion), channel_id=1, replica_groups=mesh['slab'=32,'col'=4] {'col'}, dimensions={0} | all-to-all | bytes 131072 | tf_op jit(solution)/shard_map/all_to_all | solution.py:119
  456.8 56.5 %all_to_all.47 = f32[32,1,128]{2,1,0:T(1,128)S(1)} all-to-all(f32[32,1,128]{2,1,0:T(1,128)S(1)} %reshape.28), channel_id=1, replica_groups=mesh['slab'=32,'col'=4] {'slab'}, dimensions={0} | all-to-all | bytes 32768 | tf_op jit(solution)/shard_map/all_to_all | solution.py:121
  (44 shorter events, 34.1 us)
Async XLA Ops:
  0.6 8.6 %copy-start.5 = (f32[16,2,192,128]{3,2,1,0:T(8,128)S(1)}, f32[16,2,192,128]{3,2,1,0:T(8,128)}, u32[]{:S(2)}) copy-start(f32[16,2,192,128]{3,2,1,0:T(8,128)} %param.6) | copy-start | bytes 9437188
  14.3 4.6 copy-start.1
  14.3 11.4 %copy-start.7 = (f32[8]{0:T(128)S(1)}, f32[8]{0:T(128)}, u32[]{:S(2)}) copy-start(f32[8]{0:T(128)} %param.8) | copy-start | bytes 100
  14.4 12.1 %copy-start.6 = (s32[2,192,128]{2,1,0:T(8,128)S(1)}, s32[2,192,128]{2,1,0:T(8,128)}, u32[]{:S(2)}) copy-start(s32[2,192,128]{2,1,0:T(8,128)} %param.7) | copy-start | bytes 589828
  18.9 42.5 %collective-permute-start.1 = (f32[32,1,192,128]{3,2,1,0:T(8,128)}, f32[32,1,192,128]{3,2,1,0:T(8,128)}, u32[]{:S(2)}, u32[]{:S(2)}) collective-permute-start(f32[32,1,192,128]{3,2,1,0:T(8,128)} %get-tuple-element.22), channel_id=1, source_target_pairs={{4,0},{8,4},{12,8},{16,12},{20,16},{24,20},{28,24},{32,28},{36,32}... | collective-permute-start | bytes 9437192 | tf_op jit(solution)/shard_map/ppermute | solution.py:19
  22.3 39.2 %collective-permute-start.3 = (f32[32,1,192,128]{3,2,1,0:T(8,128)}, f32[32,1,192,128]{3,2,1,0:T(8,128)}, u32[]{:S(2)}, u32[]{:S(2)}) collective-permute-start(f32[32,1,192,128]{3,2,1,0:T(8,128)} %get-tuple-element.23), channel_id=1, source_target_pairs={{0,4},{4,8},{8,12},{12,16},{16,20},{20,24},{24,28},{28,32},{32,36}... | collective-permute-start | bytes 9437192 | tf_op jit(solution)/shard_map/ppermute | solution.py:16
  31.5 28.5 %collective-permute-start = (f32[1,192,128]{2,1,0:T(8,128)S(1)}, f32[1,192,128]{2,1,0:T(8,128)S(1)}, u32[]{:S(2)}, u32[]{:S(2)}) collective-permute-start(f32[1,192,128]{2,1,0:T(8,128)S(1)} %get-tuple-element.30), channel_id=1, source_target_pairs={{4,0},{8,4},{12,8},{16,12},{20,16},{24,20},{28,24},{32,28},{36,32}... | collective-permute-start | bytes 294920 | tf_op jit(solution)/shard_map/ppermute | solution.py:19
  34.0 27.2 %collective-permute-start.2 = (f32[1,192,128]{2,1,0:T(8,128)S(1)}, f32[1,192,128]{2,1,0:T(8,128)S(1)}, u32[]{:S(2)}, u32[]{:S(2)}) collective-permute-start(f32[1,192,128]{2,1,0:T(8,128)S(1)} %get-tuple-element.31), channel_id=1, source_target_pairs={{0,4},{4,8},{8,12},{12,16},{16,20},{20,24},{24,28},{28,32},{32,36}... | collective-permute-start | bytes 294920 | tf_op jit(solution)/shard_map/ppermute | solution.py:16
  84.8 4.6 copy-start.3
  89.4 39.6 %collective-permute-start.4 = (f32[32,1,192,128]{3,2,1,0:T(8,128)}, f32[32,1,192,128]{3,2,1,0:T(8,128)}, u32[]{:S(2)}, u32[]{:S(2)}) collective-permute-start(f32[32,1,192,128]{3,2,1,0:T(8,128)} %get-tuple-element.20), channel_id=1, source_target_pairs={{4,0},{8,4},{12,8},{16,12},{20,16},{24,20},{28,24},{32,28},{36,32}... | collective-permute-start | bytes 9437192 | tf_op jit(solution)/shard_map/ppermute | solution.py:19
  91.3 38.9 %collective-permute-start.5 = (f32[32,1,192,128]{3,2,1,0:T(8,128)}, f32[32,1,192,128]{3,2,1,0:T(8,128)}, u32[]{:S(2)}, u32[]{:S(2)}) collective-permute-start(f32[32,1,192,128]{3,2,1,0:T(8,128)} %get-tuple-element.21), channel_id=1, source_target_pairs={{0,4},{4,8},{8,12},{12,16},{16,20},{20,24},{24,28},{28,32},{32,36}... | collective-permute-start | bytes 9437192 | tf_op jit(solution)/shard_map/ppermute | solution.py:16
  156.1 4.6 copy-start.2
  160.7 39.6 %collective-permute-start.6 = (f32[32,1,192,128]{3,2,1,0:T(8,128)}, f32[32,1,192,128]{3,2,1,0:T(8,128)}, u32[]{:S(2)}, u32[]{:S(2)}) collective-permute-start(f32[32,1,192,128]{3,2,1,0:T(8,128)} %get-tuple-element.18), channel_id=1, source_target_pairs={{4,0},{8,4},{12,8},{16,12},{20,16},{24,20},{28,24},{32,28},{36,32}... | collective-permute-start | bytes 9437192 | tf_op jit(solution)/shard_map/ppermute | solution.py:19
  162.6 38.9 %collective-permute-start.7 = (f32[32,1,192,128]{3,2,1,0:T(8,128)}, f32[32,1,192,128]{3,2,1,0:T(8,128)}, u32[]{:S(2)}, u32[]{:S(2)}) collective-permute-start(f32[32,1,192,128]{3,2,1,0:T(8,128)} %get-tuple-element.19), channel_id=1, source_target_pairs={{0,4},{4,8},{8,12},{12,16},{16,20},{20,24},{24,28},{28,32},{32,36}... | collective-permute-start | bytes 9437192 | tf_op jit(solution)/shard_map/ppermute | solution.py:16
  228.1 4.6 copy-start
  232.7 39.6 %collective-permute-start.8 = (f32[32,1,192,128]{3,2,1,0:T(8,128)}, f32[32,1,192,128]{3,2,1,0:T(8,128)}, u32[]{:S(2)}, u32[]{:S(2)}) collective-permute-start(f32[32,1,192,128]{3,2,1,0:T(8,128)} %get-tuple-element.15), channel_id=1, source_target_pairs={{4,0},{8,4},{12,8},{16,12},{20,16},{24,20},{28,24},{32,28},{36,32}... | collective-permute-start | bytes 9437192 | tf_op jit(solution)/shard_map/ppermute | solution.py:19
  234.6 38.9 %collective-permute-start.9 = (f32[32,1,192,128]{3,2,1,0:T(8,128)}, f32[32,1,192,128]{3,2,1,0:T(8,128)}, u32[]{:S(2)}, u32[]{:S(2)}) collective-permute-start(f32[32,1,192,128]{3,2,1,0:T(8,128)} %get-tuple-element.16), channel_id=1, source_target_pairs={{0,4},{4,8},{8,12},{12,16},{16,20},{20,24},{24,28},{28,32},{32,36}... | collective-permute-start | bytes 9437192 | tf_op jit(solution)/shard_map/ppermute | solution.py:16
  273.5 27.1 %copy-start.4 = (f32[1,32,2,192,128]{4,3,2,1,0:T(8,128)S(1)}, f32[1,32,2,192,128]{4,3,2,1,0:T(8,128)}, u32[]{:S(2)}) copy-start(f32[1,32,2,192,128]{4,3,2,1,0:T(8,128)} %get-tuple-element.17) | copy-start | bytes 18874372
  311.2 66.6 %all-to-all-start.1 = ((f32[2,16,2,192,128]{4,2,1,0,3:T(2,128)}), f32[2,16,2,192,128]{4,2,1,0,3:T(2,128)}, u32[]{:S(2)}, u32[]{:S(2)}) async-start(f32[2,16,2,192,128]{4,2,1,0,3:T(2,128)} %copy.35), calls=%async_computation.1 | async-start | bytes 12582912 | tf_op jit(solution)/shard_map/all_to_all | solution.py:100
  377.8 47.3 %all-to-all-start = ((f32[2,16,2,192,128]{4,2,1,0,3:T(2,128)}), f32[2,16,2,192,128]{4,2,1,0,3:T(2,128)}, u32[]{:S(2)}, u32[]{:S(2)}) async-start(f32[2,16,2,192,128]{4,2,1,0,3:T(2,128)} %copy.33), calls=%async_computation | async-start | bytes 12582912 | tf_op jit(solution)/shard_map/all_to_all | solution.py:99
where the time goes:
time: 517 us; the launch traced here: 515 us
  waiting for transfers between devices  198 us (38%)
  other arithmetic  118 us (23%)
  local copies, waits for them, and re-layouts  77.1 us (15%)
  blocking collectives  63.4 us (12%)
  starting transfers between devices  42.2 us (8%)
  between operations  8.77 us (2%)
  matrix products  8.21 us (2%)
    ppermute x5, waiting for transfers between devices, extended(): lax.ppermute(lax.slice_in_dim(block, 0, width, axis=dim), axis, backward)  117 us
    all_to_all x1, blocking collectives, body(): lax.all_to_all(row_parts, 'slab', 0, 0, tiled=True)  56.5 us
    all_to_all x1, waiting for transfers between devices, body(): lax.all_to_all(obsv_local, 'col', split_axis=3, concat_axis=1, tiled=True)  51 us
    add x2, other arithmetic, solve_slabs(): rho_next * rho_now * direction + 2.0 * rho_next / half_span * residual  49.9 us
    another operation x2, other arithmetic, run_segments(): return jnp.stack(factors)  30.2 us
    div x2, other arithmetic, solve_slabs(): direction = right_side / mid_eig  29.1 us
    all_to_all x1, waiting for transfers between devices, body(): lax.all_to_all(ctrl_local, 'col', split_axis=3, concat_axis=1, tiled=True)  25.4 us
    ppermute x5, starting transfers between devices, extended(): lax.ppermute(lax.slice_in_dim(block, block.shape[dim] - width, None, axis...  19.9 us
  transfers between devices with their start and end apart: 12, of which 10 were waited for; matrix products, arithmetic and copies ran while one was open for 6% of the time, Pallas kernels for 0%

commit v1 on v0

--- a/solution.py
+++ b/solution.py
@@ -97,7 +97,12 @@
     obsv_local = factor_stack[:, col_local:]
     ctrl_cols, obsv_cols = (
         lax.all_to_all(ctrl_local, "col", split_axis=3, concat_axis=1, tiled=True),
-        lax.all_to_all(obsv_local, "col", split_axis=3, concat_axis=1, tiled=True),
+        jnp.concatenate(
+            lax.all_to_all(
+                jnp.stack(jnp.split(obsv_local, lax.axis_size("col"), axis=3)), "col", 0, 0
+            ),
+            axis=1,
+        ),
     )
     row_count = ctrl_cols.shape[0] * ctrl_cols.shape[1]
     ctrl_flat = ctrl_cols.reshape(row_count, -1)

time: 517 us -> 512 us (level)
  local copies, waits for them, and re-layouts: 77.1 us -> 65.6 us
    slice x1 -> x0, local copies, waits for them, and re-layouts: 7.51 us -> none  [body(): obsv_local = factor_stack[:, col_local:]]
    unnamed x19 -> x23, local copies, waits for them, and re-layouts: 8.25 us -> 10.6 us
where the time goes in v1:
time: 512 us; the launch traced here: 510 us
  waiting for transfers between devices  201 us (39%)
  other arithmetic  122 us (24%)
  local copies, waits for them, and re-layouts  65.6 us (13%)
  blocking collectives  63.4 us (12%)
  starting transfers between devices  42.2 us (8%)
  between operations  8.59 us (2%)
  matrix products  8.21 us (2%)
    ppermute x5, waiting for transfers between devices, extended(): lax.ppermute(lax.slice_in_dim(block, 0, width, axis=dim), axis, backward)  117 us
    all_to_all x1, blocking collectives, body(): lax.all_to_all(row_parts, 'slab', 0, 0, tiled=True)  56.5 us
    all_to_all x1, waiting for transfers between devices, body(): lax.all_to_all(jnp.stack(jnp.split(obsv_local, lax.axis_size('col'), axis...  50.5 us
    add x2, other arithmetic, solve_slabs(): rho_next * rho_now * direction + 2.0 * rho_next / half_span * residual  49.9 us
    another operation x2, other arithmetic, run_segments(): return jnp.stack(factors)  30.3 us
    div x2, other arithmetic, solve_slabs(): direction = right_side / mid_eig  29.2 us
    all_to_all x1, waiting for transfers between devices, body(): lax.all_to_all(ctrl_local, 'col', split_axis=3, concat_axis=1, tiled=True)  28.5 us
    ppermute x5, starting transfers between devices, extended(): lax.ppermute(lax.slice_in_dim(block, block.shape[dim] - width, None, axis...  19.9 us
  transfers between devices with their start and end apart: 12, of which 10 were waited for; matrix products, arithmetic and copies ran while one was open for 6% of the time, Pallas kernels for 0%

profile of v1, /device:TPU:1, one launch (start us, length us, event | category | flops | bytes accessed | tf_op | source)
XLA Modules:
  0.0 510.5 jit_solution(9974145277832924490)
XLA Ops:
  5.3 3.9 constant_dynamic-update-slice_fusion.1
  14.4 3.3 fusion.112
  18.9 3.3 collective-permute-start.1
  22.3 3.5 collective-permute-start.3
  26.5 5.0 select_add_fusion
  37.9 22.2 %collective-permute-done = f32[1,192,128]{2,1,0:T(8,128)S(1)} collective-permute-done((f32[1,192,128]{2,1,0:T(8,128)S(1)}, f32[1,192,128]{2,1,0:T(8,128)S(1)}, u32[]{:S(2)}, u32[]{:S(2)}) %collective-permute-start) | collective-permute-done | bytes 98336 | tf_op jit(solution)/shard_map/ppermute | solution.py:19
  61.4 23.3 %multiply_add_fusion.1 = (f32[32,2,192,128]{3,2,1,0:T(8,128)S(1)}, f32[32,2,192,128]{3,2,1,0:T(8,128)}) fusion(f32[32,2,192,128]{3,2,1,0:T(8,128)} %copy-done.2, f32[]{:T(128)S(6)} %div.53, f32[]{:T(128)S(6)} %mul.348, f32[32,2,192,128]{3,2,1,0:T(8,128)} %constant_dynamic-update-slice_fusion, f32[]{:T(128)} %bitcast, ...), kind=kLoop, calls=%fused_computation.122 | loop fusion | flops 39321600 | bytes 32636940 | tf_op jit(solution)/shard_map/add | solution.py:66
  84.8 3.3 fusion.111
  91.3 4.4 collective-permute-start.5
  97.0 32.0 %collective-permute-done.4 = f32[32,1,192,128]{3,2,1,0:T(8,128)} collective-permute-done((f32[32,1,192,128]{3,2,1,0:T(8,128)}, f32[32,1,192,128]{3,2,1,0:T(8,128)}, u32[]{:S(2)}, u32[]{:S(2)}) %collective-permute-start.4) | collective-permute-done | bytes 3145760 | tf_op jit(solution)/shard_map/ppermute | solution.py:19
  130.2 25.9 %broadcast_divide_fusion = (f32[32,2,192,128]{3,2,1,0:T(8,128)S(1)}, f32[32,2,192,128]{3,2,1,0:T(8,128)}) fusion(f32[]{:T(128)S(6)} %mul.391, f32[32,2,192,128]{3,2,1,0:T(8,128)} %get-tuple-element.8, f32[32,2,192,128]{3,2,1,0:T(8,128)} %copy-done.4, f32[]{:T(128)} %bitcast, f32[2,192,128]{2,1,0:T(8,128)S(1)} %get-tuple-element.31, ...), kind=kLoop, calls=%fused_computation.123 | loop fusion | flops 45613056 | bytes 38928404 | tf_op jit(solution)/shard_map/div | solution.py:59
  156.1 3.8 fusion.110
  162.6 4.4 collective-permute-start.7
  168.5 31.8 %collective-permute-done.6 = f32[32,1,192,128]{3,2,1,0:T(8,128)} collective-permute-done((f32[32,1,192,128]{3,2,1,0:T(8,128)}, f32[32,1,192,128]{3,2,1,0:T(8,128)}, u32[]{:S(2)}, u32[]{:S(2)}) %collective-permute-start.6) | collective-permute-done | bytes 3145760 | tf_op jit(solution)/shard_map/ppermute | solution.py:19
  201.5 26.5 %multiply_add_fusion = (f32[32,2,192,128]{3,2,1,0:T(8,128)S(1)}, f32[32,2,192,128]{3,2,1,0:T(8,128)}, f32[1,32,2,192,128]{4,3,2,1,0:T(8,128)}) fusion(f32[]{:T(128)S(6)} %div.61, f32[]{:T(128)S(6)} %mul.394, f32[32,2,192,128]{3,2,1,0:T(8,128)} %get-tuple-element.6, f32[]{:T(128)S(6)} %mul.391, f32[32,2,192,128]{3,2,1,0:T(8,128)} %copy-done.3, f32[]{:T(128)} %bitcast.10, ...), kind=kLoop, calls=%fused_computation.120 | loop fusion | flops 42467328 | bytes 38928404 | tf_op jit(solution)/shard_map/add | solution.py:66
  228.1 3.4 fusion.109
  234.8 4.6 collective-permute-start.9
  241.4 31.1 %collective-permute-done.8 = f32[32,1,192,128]{3,2,1,0:T(8,128)} collective-permute-done((f32[32,1,192,128]{3,2,1,0:T(8,128)}, f32[32,1,192,128]{3,2,1,0:T(8,128)}, u32[]{:S(2)}, u32[]{:S(2)}) %collective-permute-start.8) | collective-permute-done | bytes 3145760 | tf_op jit(solution)/shard_map/ppermute | solution.py:19
  273.7 27.0 %fusion.47 = f32[1,32,2,192,128]{4,3,2,1,0:T(8,128)S(1)} fusion(f32[32,2,192,128]{3,2,1,0:T(8,128)} %get-tuple-element.6, f32[32,2,192,128]{3,2,1,0:T(8,128)} %get-tuple-element.4, f32[32,2,192,128]{3,2,1,0:T(8,128)} %copy-done.1, f32[32,1,192,128]{3,2,1,0:T(8,128)} %collective-permute-done.9, f32[32,1,192,128]{3,2,1,0:T(8,128)} %collective-permute-done.8, ...), kind=kLoop, calls=%fused_computation.71 | loop fusion | flops 48758784 | bytes 32636952 | tf_op jit(solution)/shard_map/stack | solution.py:81
  306.4 5.2 %all-to-all-start.1 = ((f32[4,2,16,2,48,128]{5,4,3,2,1,0:T(8,128)}), f32[4,2,16,2,48,128]{5,4,3,2,1,0:T(8,128)}, u32[]{:S(2)}, u32[]{:S(2)}) async-start(f32[4,2,16,2,48,128]{5,4,3,2,1,0:T(8,128)} %pad_maximum_fusion.8), calls=%async_computation.1 | async-start | bytes 12582912 | tf_op jit(solution)/shard_map/all_to_all | solution.py:101
  311.6 3.3 fusion.66
  314.9 7.6 %copy.41 = f32[2,16,2,192,128]{4,2,1,0,3:T(2,128)} copy(f32[2,16,2,192,128]{4,3,2,1,0:T(8,128)S(1)} %fusion.66) | data formatting | bytes 12582912 | tf_op jit(solution)/shard_map/slice | solution.py:96
  322.4 50.5 %all-to-all-done.1 = f32[4,2,16,2,48,128]{5,4,3,2,1,0:T(8,128)} async-done(((f32[4,2,16,2,48,128]{5,4,3,2,1,0:T(8,128)}), f32[4,2,16,2,48,128]{5,4,3,2,1,0:T(8,128)}, u32[]{:S(2)}, u32[]{:S(2)}) %all-to-all-start.1) | async-done | bytes 6291488 | tf_op jit(solution)/shard_map/all_to_all | solution.py:101
  372.9 5.5 %all-to-all-start = ((f32[2,16,2,192,128]{4,2,1,0,3:T(2,128)}), f32[2,16,2,192,128]{4,2,1,0,3:T(2,128)}, u32[]{:S(2)}, u32[]{:S(2)}) async-start(f32[2,16,2,192,128]{4,2,1,0,3:T(2,128)} %copy.41), calls=%async_computation | async-start | bytes 12582912 | tf_op jit(solution)/shard_map/all_to_all | solution.py:99
  378.4 5.9 %copy.49 = f32[4,2,16,2,48,128]{5,4,3,2,0,1:T(8,128)} copy(f32[4,2,16,2,48,128]{5,4,3,2,1,0:T(8,128)} %all-to-all-done.1) | data formatting | bytes 12582912 | tf_op jit(solution)/shard_map/all_to_all | solution.py:101
  384.3 7.4 %dot_general.5 = f32[4,32,12288]{2,1,0:T(8,128)} reshape(f32[2,4,16,2,48,128]{5,4,3,2,1,0:T(8,128)} %bitcast.44) | data formatting | bytes 12582912 | tf_op jit(solution)/shard_map/dot_general | solution.py:110
  391.7 28.5 %all-to-all-done = f32[2,16,2,192,128]{4,2,1,0,3:T(2,128)} async-done(((f32[2,16,2,192,128]{4,2,1,0,3:T(2,128)}), f32[2,16,2,192,128]{4,2,1,0,3:T(2,128)}, u32[]{:S(2)}, u32[]{:S(2)}) %all-to-all-start) | async-done | bytes 6291488 | tf_op jit(solution)/shard_map/all_to_all | solution.py:99
  420.2 9.0 %copy.50 = f32[2,16,2,4,48,128]{5,4,2,1,3,0:T(8,128)} copy(f32[2,16,2,4,48,128]{5,2,1,0,4,3:T(2,128)} %bitcast.12) | data formatting | bytes 12582912 | tf_op jit(solution)/shard_map/all_to_all | solution.py:99
  429.2 7.5 %reshape.32 = f32[128,12288,1]{1,0,2:T(8,128)} reshape(f32[2,4,16,2,48,128]{5,4,3,2,1,0:T(8,128)} %bitcast.46) | data formatting | bytes 12582912 | tf_op jit(solution)/shard_map/reshape | solution.py:108
  436.7 8.2 %convolution_bitcast_fusion = f32[4,128,32]{1,2,0:T(8,128)S(1)} fusion(f32[128,12288,1]{1,0,2:T(8,128)} %reshape.32, f32[4,32,12288]{2,1,0:T(8,128)} %dot_general.5), kind=kOutput, calls=%fused_computation.133 | convolution fusion | flops 2415919104 | bytes 12648448 | tf_op jit(solution)/shard_map/dot_general | solution.py:110
  444.9 6.8 %all_to_all.33 = f32[4,128,32]{1,2,0:T(8,128)S(1)} all-to-all(f32[4,128,32]{1,2,0:T(8,128)S(1)} %convolution_bitcast_fusion), channel_id=1, replica_groups=mesh['slab'=32,'col'=4] {'col'}, dimensions={0} | all-to-all | bytes 131072 | tf_op jit(solution)/shard_map/all_to_all | solution.py:124
  452.0 56.5 %all_to_all.34 = f32[32,1,128]{2,1,0:T(1,128)S(1)} all-to-all(f32[32,1,128]{2,1,0:T(1,128)S(1)} %reshape.34), channel_id=1, replica_groups=mesh['slab'=32,'col'=4] {'slab'}, dimensions={0} | all-to-all | bytes 32768 | tf_op jit(solution)/shard_map/all_to_all | solution.py:126
  (50 shorter events, 37.2 us)
Async XLA Ops:
  0.6 8.6 %copy-start.5 = (f32[16,2,192,128]{3,2,1,0:T(8,128)S(1)}, f32[16,2,192,128]{3,2,1,0:T(8,128)}, u32[]{:S(2)}) copy-start(f32[16,2,192,128]{3,2,1,0:T(8,128)} %param.6) | copy-start | bytes 9437188
  14.3 4.6 copy-start.2
  14.3 11.4 %copy-start.7 = (f32[8]{0:T(128)S(1)}, f32[8]{0:T(128)}, u32[]{:S(2)}) copy-start(f32[8]{0:T(128)} %param.8) | copy-start | bytes 100
  14.4 12.1 %copy-start.6 = (s32[2,192,128]{2,1,0:T(8,128)S(1)}, s32[2,192,128]{2,1,0:T(8,128)}, u32[]{:S(2)}) copy-start(s32[2,192,128]{2,1,0:T(8,128)} %param.7) | copy-start | bytes 589828
  18.9 42.5 %collective-permute-start.1 = (f32[32,1,192,128]{3,2,1,0:T(8,128)}, f32[32,1,192,128]{3,2,1,0:T(8,128)}, u32[]{:S(2)}, u32[]{:S(2)}) collective-permute-start(f32[32,1,192,128]{3,2,1,0:T(8,128)} %get-tuple-element.24), channel_id=1, source_target_pairs={{4,0},{8,4},{12,8},{16,12},{20,16},{24,20},{28,24},{32,28},{36,32}... | collective-permute-start | bytes 9437192 | tf_op jit(solution)/shard_map/ppermute | solution.py:19
  22.3 39.2 %collective-permute-start.3 = (f32[32,1,192,128]{3,2,1,0:T(8,128)}, f32[32,1,192,128]{3,2,1,0:T(8,128)}, u32[]{:S(2)}, u32[]{:S(2)}) collective-permute-start(f32[32,1,192,128]{3,2,1,0:T(8,128)} %get-tuple-element.25), channel_id=1, source_target_pairs={{0,4},{4,8},{8,12},{12,16},{16,20},{20,24},{24,28},{28,32},{32,36}... | collective-permute-start | bytes 9437192 | tf_op jit(solution)/shard_map/ppermute | solution.py:16
  31.5 28.6 %collective-permute-start = (f32[1,192,128]{2,1,0:T(8,128)S(1)}, f32[1,192,128]{2,1,0:T(8,128)S(1)}, u32[]{:S(2)}, u32[]{:S(2)}) collective-permute-start(f32[1,192,128]{2,1,0:T(8,128)S(1)} %get-tuple-element.32), channel_id=1, source_target_pairs={{4,0},{8,4},{12,8},{16,12},{20,16},{24,20},{28,24},{32,28},{36,32}... | collective-permute-start | bytes 294920 | tf_op jit(solution)/shard_map/ppermute | solution.py:19
  34.0 27.2 %collective-permute-start.2 = (f32[1,192,128]{2,1,0:T(8,128)S(1)}, f32[1,192,128]{2,1,0:T(8,128)S(1)}, u32[]{:S(2)}, u32[]{:S(2)}) collective-permute-start(f32[1,192,128]{2,1,0:T(8,128)S(1)} %get-tuple-element.33), channel_id=1, source_target_pairs={{0,4},{4,8},{8,12},{12,16},{16,20},{20,24},{24,28},{28,32},{32,36}... | collective-permute-start | bytes 294920 | tf_op jit(solution)/shard_map/ppermute | solution.py:16
  84.8 4.6 copy-start.4
  89.4 39.6 %collective-permute-start.4 = (f32[32,1,192,128]{3,2,1,0:T(8,128)}, f32[32,1,192,128]{3,2,1,0:T(8,128)}, u32[]{:S(2)}, u32[]{:S(2)}) collective-permute-start(f32[32,1,192,128]{3,2,1,0:T(8,128)} %get-tuple-element.22), channel_id=1, source_target_pairs={{4,0},{8,4},{12,8},{16,12},{20,16},{24,20},{28,24},{32,28},{36,32}... | collective-permute-start | bytes 9437192 | tf_op jit(solution)/shard_map/ppermute | solution.py:19
  91.3 38.9 %collective-permute-start.5 = (f32[32,1,192,128]{3,2,1,0:T(8,128)}, f32[32,1,192,128]{3,2,1,0:T(8,128)}, u32[]{:S(2)}, u32[]{:S(2)}) collective-permute-start(f32[32,1,192,128]{3,2,1,0:T(8,128)} %get-tuple-element.23), channel_id=1, source_target_pairs={{0,4},{4,8},{8,12},{12,16},{16,20},{20,24},{24,28},{28,32},{32,36}... | collective-permute-start | bytes 9437192 | tf_op jit(solution)/shard_map/ppermute | solution.py:16
  156.1 4.6 copy-start.3
  160.7 39.6 %collective-permute-start.6 = (f32[32,1,192,128]{3,2,1,0:T(8,128)}, f32[32,1,192,128]{3,2,1,0:T(8,128)}, u32[]{:S(2)}, u32[]{:S(2)}) collective-permute-start(f32[32,1,192,128]{3,2,1,0:T(8,128)} %get-tuple-element.20), channel_id=1, source_target_pairs={{4,0},{8,4},{12,8},{16,12},{20,16},{24,20},{28,24},{32,28},{36,32}... | collective-permute-start | bytes 9437192 | tf_op jit(solution)/shard_map/ppermute | solution.py:19
  162.6 38.9 %collective-permute-start.7 = (f32[32,1,192,128]{3,2,1,0:T(8,128)}, f32[32,1,192,128]{3,2,1,0:T(8,128)}, u32[]{:S(2)}, u32[]{:S(2)}) collective-permute-start(f32[32,1,192,128]{3,2,1,0:T(8,128)} %get-tuple-element.21), channel_id=1, source_target_pairs={{0,4},{4,8},{8,12},{12,16},{16,20},{20,24},{24,28},{28,32},{32,36}... | collective-permute-start | bytes 9437192 | tf_op jit(solution)/shard_map/ppermute | solution.py:16
  228.1 4.7 copy-start.1
  228.1 72.6 %slice-start = ((s8[6291456]{0:T(1024)(128)(4,1)}), s8[2097152]{0:T(1024)(128)(4,1)S(1)}, s32[]{:S(2)}) async-start(s8[6291456]{0:T(1024)(128)(4,1)} %bitcast.42), calls=%async_computation.4 | async-start | bytes 4194304
  232.8 39.6 %collective-permute-start.8 = (f32[32,1,192,128]{3,2,1,0:T(8,128)}, f32[32,1,192,128]{3,2,1,0:T(8,128)}, u32[]{:S(2)}, u32[]{:S(2)}) collective-permute-start(f32[32,1,192,128]{3,2,1,0:T(8,128)} %get-tuple-element.17), channel_id=1, source_target_pairs={{4,0},{8,4},{12,8},{16,12},{20,16},{24,20},{28,24},{32,28},{36,32}... | collective-permute-start | bytes 9437192 | tf_op jit(solution)/shard_map/ppermute | solution.py:19
  234.8 38.9 %collective-permute-start.9 = (f32[32,1,192,128]{3,2,1,0:T(8,128)}, f32[32,1,192,128]{3,2,1,0:T(8,128)}, u32[]{:S(2)}, u32[]{:S(2)}) collective-permute-start(f32[32,1,192,128]{3,2,1,0:T(8,128)} %get-tuple-element.18), channel_id=1, source_target_pairs={{0,4},{4,8},{8,12},{12,16},{16,20},{20,24},{24,28},{28,32},{32,36}... | collective-permute-start | bytes 9437192 | tf_op jit(solution)/shard_map/ppermute | solution.py:16
  273.7 27.1 %slice-start.1 = ((s8[6291456]{0:T(1024)(128)(4,1)}), s8[4194304]{0:T(1024)(128)(4,1)S(1)}, s32[]{:S(2)}) async-start(s8[6291456]{0:T(1024)(128)(4,1)} %bitcast.42), calls=%async_computation.5 | async-start | bytes 8388608
  300.7 2.8 copy-start
  306.4 66.5 %all-to-all-start.1 = ((f32[4,2,16,2,48,128]{5,4,3,2,1,0:T(8,128)}), f32[4,2,16,2,48,128]{5,4,3,2,1,0:T(8,128)}, u32[]{:S(2)}, u32[]{:S(2)}) async-start(f32[4,2,16,2,48,128]{5,4,3,2,1,0:T(8,128)} %pad_maximum_fusion.8), calls=%async_computation.1 | async-start | bytes 12582912 | tf_op jit(solution)/shard_map/all_to_all | solution.py:101
  372.9 47.3 %all-to-all-start = ((f32[2,16,2,192,128]{4,2,1,0,3:T(2,128)}), f32[2,16,2,192,128]{4,2,1,0,3:T(2,128)}, u32[]{:S(2)}, u32[]{:S(2)}) async-start(f32[2,16,2,192,128]{4,2,1,0,3:T(2,128)} %copy.41), calls=%async_computation | async-start | bytes 12582912 | tf_op jit(solution)/shard_map/all_to_all | solution.py:99
